TPU v7x, 32 devices: a whole 2x2x4 slice. The times are simulated.
32 devices in a mesh: grp: 2 (over y), rows: 4 (over z), img: 2 (over x), tp: 2 (over core).
Axes of the slice: x: 2, y: 2, z: 4, core: 2. Of those that a mesh axis runs over, the one named last changes fastest.
Arguments:
- features: bfloat16 [16, 28, 2, 7168], P(('grp', 'img'), 'rows', 'tp'), parts along dimension 0, may hold values from -8 to 8
- gn_gain: float32 [128], P('tp'), may hold values from 0.5 to 1.5
- conv_w: bfloat16 [3, 3, 3, 128], P(None, None, None, 'tp'), may hold values from -0.1875 to 0.1875
- patch_w: bfloat16 [1280, 588], P('rows'), may hold values from -0.25 to 0.25
- pos_emb: bfloat16 [64, 1280], replicated, may hold values from -3 to 3
- ln1_gain: float32 [1280], replicated, may hold values from 0.5 to 1.5
- qkv_w: bfloat16 [1280, 3, 1280], P('rows', None, 'tp'), may hold values from -3 to 3
- out_w: bfloat16 [1280, 1280], P('rows', 'tp'), may hold values from -0.15625 to 0.15625
- final_gain: float32 [1280], replicated, may hold values from 0.5 to 1.5
- head_w: float32 [1280], replicated, may hold values from -0.15625 to 0.15625
- owner_slot: int32 [4, 4], P(('grp', 'img')), parts along dimension 0, may hold values from 0 to 3, each once within a row
Outputs:
- grad_features: bfloat16 [16, 28, 2, 7168], P(('grp', 'img'), 'rows', 'tp'), parts along dimension 0
- slot_reward: float32 [16], P(('grp', 'img', 'rows')), parts along dimension 0
There are 2 independent parts, one for each index of `grp`. A program takes and returns all parts, laid end to end along the dimension named above; an argument that names none is the same for every part. Nothing has to cross between parts.
Inputs may be any that keep to these rules, and one draw needn't show every extreme that they name: Each row is a permutation: image g * 4 + j is scored in slot owner_slot[g, j] of its image group.
All inputs are finite; a program needn't handle non-finite values.
Results may differ from a plain program's by a relative error of at most 0.028.
Values may be sent and summed in bfloat16 or wider, within the bound.
A program may use at most 128 MiB of HBM per device.

v0:
```python
import math
import jax
import jax.numpy as jnp
from jax import lax
from jax.sharding import PartitionSpec as P

C = 128
GROUPS = 32
PATCH = 14
HEAD_DIM = 80
W = 112
EPS_GROUP = 1e-06
EPS_LAYER = 1e-05


def padded_2(block, sides, width):
    for axis, dim in sides:
        count = lax.axis_size(axis)
        forward = [(i, i + 1) for i in range(count - 1)]
        backward = [(target, source) for source, target in forward]
        low = lax.ppermute(
            lax.slice_in_dim(block, block.shape[dim] - width, None, axis=dim), axis, forward
        )
        high = lax.ppermute(lax.slice_in_dim(block, 0, width, axis=dim), axis, backward)
        block = jnp.concatenate([low, block, high], axis=dim)
    return block


def round_half(values):
    return lax.optimization_barrier(values.astype(jnp.bfloat16)).astype(jnp.float32)


def layer_norm(values, scale_vec):
    average = jnp.mean(values, axis=-1, keepdims=True)
    centred = values - average
    spread = jnp.mean(centred * centred, axis=-1, keepdims=True)
    inverse = lax.rsqrt(spread + EPS_LAYER)
    normed = centred * inverse
    return (normed * scale_vec, normed, inverse)


def layer_norm_back(upstream, normed, inverse, scale_vec):
    scaled = upstream * scale_vec
    mean_one = jnp.mean(scaled, axis=-1, keepdims=True)
    mean_two = jnp.mean(scaled * normed, axis=-1, keepdims=True)
    return inverse * (scaled - mean_one - normed * mean_two)


def silu_parts(values):
    sigmoid = jax.nn.sigmoid(values)
    return (values * sigmoid, sigmoid * (1.0 + values * (1.0 - sigmoid)))


def soft_weights(q_heads, k_heads):
    factor = 1.0 / math.sqrt(HEAD_DIM)
    scores = jnp.einsum("thd,shd->hts", q_heads, k_heads) * factor
    row_max = jnp.max(scores, axis=-1, keepdims=True)
    exp_scores = jnp.exp(scores - row_max)
    return exp_scores / jnp.sum(exp_scores, axis=-1, keepdims=True)


def split_heads(rows_in):
    return rows_in.reshape(rows_in.shape[0], rows_in.shape[1] // HEAD_DIM, HEAD_DIM).astype(
        jnp.float32
    )


def attend(queries, key_rows, value_rows):
    prob_soft = soft_weights(split_heads(queries), split_heads(key_rows))
    attended = jnp.einsum("hts,shd->thd", round_half(prob_soft), split_heads(value_rows))
    return attended.reshape(queries.shape).astype(jnp.bfloat16)


def attend_back(queries, key_rows, value_rows, head_grad):
    factor = 1.0 / math.sqrt(HEAD_DIM)
    q_heads = split_heads(queries)
    k_heads = split_heads(key_rows)
    v_heads = split_heads(value_rows)
    g_heads = split_heads(head_grad)
    prob_soft = soft_weights(q_heads, k_heads)
    dprob = jnp.einsum("thd,shd->hts", g_heads, v_heads)
    dvalue = (
        jnp.einsum("hts,thd->shd", round_half(prob_soft), g_heads)
        .reshape(queries.shape)
        .astype(jnp.bfloat16)
    )
    dscores = prob_soft * (dprob - jnp.sum(dprob * prob_soft, axis=-1, keepdims=True)) * factor
    dscores = round_half(dscores)
    dquery = (
        jnp.einsum("hts,shd->thd", dscores, k_heads).reshape(queries.shape).astype(jnp.bfloat16)
    )
    dkey = jnp.einsum("hts,thd->shd", dscores, q_heads).reshape(queries.shape).astype(jnp.bfloat16)
    return (dquery, dkey, dvalue)


def rows_total_sum(values):
    return lax.psum(values, "rows")


def head_total(values):
    return lax.psum(values.astype(jnp.bfloat16), "tp").astype(jnp.float32)


def regroup(values):
    return lax.all_to_all(values, "rows", split_axis=0, concat_axis=0, tiled=True)


def body(
    features,
    gn_gain,
    conv_w,
    patch_w,
    pos_emb,
    ln1_gain,
    qkv_w,
    out_w,
    final_gain,
    head_w,
    owner_slot,
):
    slab_imgs, rows_here, _, flat_width = features.shape
    col_count = W
    chan_count = flat_width // col_count
    row_devices = lax.axis_size("rows")
    rows_total = rows_here * row_devices
    groups_here = GROUPS * chan_count // C
    group_width = chan_count // groups_here
    count_group = rows_total * col_count * group_width
    own_count = slab_imgs // row_devices
    half_patch = PATCH // 2
    patch_rows = rows_total // half_patch
    patch_cols = col_count // half_patch

    def channel_group_sums(flat):
        per_col = jnp.sum(flat, axis=1).reshape(slab_imgs, col_count, chan_count)
        per_chan = jnp.sum(per_col, axis=1)
        return jnp.sum(per_chan.reshape(slab_imgs, groups_here, group_width), axis=2)

    def spread_flat(per_group):
        return jnp.tile(jnp.repeat(per_group, group_width, axis=1), (1, col_count))[:, None, :]

    feat_float = features.reshape(slab_imgs, rows_here, flat_width).astype(jnp.float32)
    stat_sums = rows_total_sum(
        jnp.stack([channel_group_sums(feat_float), channel_group_sums(feat_float * feat_float)])
    )
    average = stat_sums[0] / count_group
    inverse = lax.rsqrt(stat_sums[1] / count_group - average * average + EPS_GROUP)
    gain_flat = jnp.tile(gn_gain, col_count)[None, None, :]
    normed = (feat_float - spread_flat(average)) * spread_flat(inverse)
    scaled = normed * gain_flat
    active, slope_silu = silu_parts(scaled)
    active = active.astype(jnp.bfloat16)
    kernel_rows = conv_w.reshape(27, chan_count)
    widened = jnp.pad(active, ((0, 0), (2, 2), (0, 0)))
    block_rows = widened.shape[1]
    padded = jnp.pad(widened, ((0, 0), (0, 0), (chan_count, chan_count)))
    terms = lax.dot_general(
        kernel_rows,
        padded.reshape(-1, chan_count),
        (((1,), (1,)), ((), ())),
        preferred_element_type=jnp.float32,
    )
    shifted_terms = terms.reshape(3, 3, 3, slab_imgs, block_rows, col_count + 2)
    out_rows = rows_here + 2
    total = jnp.zeros((3, slab_imgs, out_rows, col_count), jnp.float32)
    for shifted_offset_y in range(3):
        for shifted_offset_x in range(3):
            total = (
                total
                + shifted_terms[
                    :,
                    shifted_offset_y,
                    shifted_offset_x,
                    :,
                    shifted_offset_y : shifted_offset_y + out_rows,
                    shifted_offset_x : shifted_offset_x + col_count,
                ]
            )
    edges = jnp.concatenate([total[:, :, :1], total[:, :, -1:]], axis=2)
    edges_rim = padded_2(edges, (("rows", 2),), 1)
    middle = total[:, :, 1:-1]
    partial_rgb = (
        middle.at[:, :, 0:1].add(edges_rim[:, :, 0:1]).at[:, :, -1:].add(edges_rim[:, :, 3:4])
    )
    picture = head_total(partial_rgb).astype(jnp.bfloat16)
    slot_of = owner_slot[0]
    slot_ids = jnp.arange(slab_imgs, dtype=jnp.int32)
    selector = (slot_of[None, :] == slot_ids[:, None]).astype(jnp.bfloat16)
    by_image = picture.transpose(1, 0, 2, 3).reshape(slab_imgs, -1)
    ordered = jnp.dot(selector, by_image, preferred_element_type=jnp.float32).astype(jnp.bfloat16)
    outgoing = ordered.reshape(row_devices, own_count, 3, rows_here, col_count)
    arrived = regroup(outgoing)
    owned_images = arrived.transpose(1, 2, 0, 3, 4).reshape(own_count, 3, rows_total, col_count)
    gathered = (
        lax.all_gather(qkv_w, "rows", axis=0, tiled=True),
        lax.all_gather(out_w, "rows", axis=0, tiled=True),
        lax.all_gather(patch_w, "rows", axis=0, tiled=True),
    )
    qkv_half = gathered[0]
    out_half = gathered[1]
    patch_full = gathered[2]
    entry_index = jnp.arange(3 * PATCH * PATCH, dtype=jnp.int32)
    colour = entry_index % 3
    pixel_index = entry_index // 3
    target = (
        colour * half_patch * half_patch
        + pixel_index // PATCH // 2 * half_patch
        + pixel_index % PATCH // 2
    )
    fold_table = (
        target[:, None] == jnp.arange(3 * half_patch * half_patch, dtype=jnp.int32)[None, :]
    ).astype(jnp.float32)
    folded_weight = jnp.dot(
        patch_full.astype(jnp.float32), fold_table, precision=lax.Precision.HIGHEST
    )

    def forward_one(picture_one):
        patch_cells = picture_one.reshape(
            3, patch_rows, half_patch, patch_cols, half_patch
        ).transpose(1, 3, 0, 2, 4)
        patch_cells = patch_cells.reshape(
            patch_rows * patch_cols, 3 * half_patch * half_patch
        ).astype(jnp.float32)
        embedded = jnp.dot(
            patch_cells, folded_weight.T, precision=lax.Precision.HIGHEST
        ) + pos_emb.astype(jnp.float32)
        normed_in, hat_in, inv_in = layer_norm(embedded, ln1_gain)
        normed_round = normed_in.astype(jnp.bfloat16)
        queries = jnp.dot(
            normed_round, qkv_half[:, 0, :], preferred_element_type=jnp.float32
        ).astype(jnp.bfloat16)
        key_rows = jnp.dot(
            normed_round, qkv_half[:, 1, :], preferred_element_type=jnp.float32
        ).astype(jnp.bfloat16)
        value_rows = jnp.dot(
            normed_round, qkv_half[:, 2, :], preferred_element_type=jnp.float32
        ).astype(jnp.bfloat16)
        attended = attend(queries, key_rows, value_rows)
        mixed_out = head_total(jnp.dot(attended, out_half.T, preferred_element_type=jnp.float32))
        residual_out = embedded + mixed_out
        pooled = jnp.mean(residual_out, axis=0)
        pooled_out, hat_z, inv_z = layer_norm(pooled, final_gain)
        reward = jnp.sum(pooled_out * head_w)
        return (reward, (hat_in, inv_in, queries, key_rows, value_rows, hat_z, inv_z))

    rewards, stored = lax.map(forward_one, owned_images)

    def backward_one(saved_one):
        hat_in, inv_in, queries, key_rows, value_rows, hat_z, inv_z = saved_one
        upstream = layer_norm_back(head_w, hat_z, inv_z, final_gain)
        row_round = upstream.astype(jnp.bfloat16)[None, :]
        head_grad = jnp.dot(row_round, out_half, preferred_element_type=jnp.float32).astype(
            jnp.bfloat16
        )
        head_grad = jnp.broadcast_to(head_grad, queries.shape)
        dquery, dkey, dvalue = attend_back(queries, key_rows, value_rows, head_grad)
        partial_value = jnp.dot(dquery, qkv_half[:, 0, :].T, preferred_element_type=jnp.float32)
        partial_value = partial_value + jnp.dot(
            dkey, qkv_half[:, 1, :].T, preferred_element_type=jnp.float32
        )
        partial_value = partial_value + jnp.dot(
            dvalue, qkv_half[:, 2, :].T, preferred_element_type=jnp.float32
        )
        dnormed = head_total(partial_value)
        dembedded = upstream[None, :] + layer_norm_back(dnormed, hat_in, inv_in, ln1_gain)
        cell_grads = jnp.dot(round_half(dembedded), folded_weight, precision=lax.Precision.HIGHEST)
        cell_grads = cell_grads.reshape(
            patch_rows, patch_cols, 3, half_patch, half_patch
        ).transpose(2, 0, 3, 1, 4)
        return cell_grads.reshape(3, rows_total, col_count).astype(jnp.bfloat16)

    back_owned = lax.map(backward_one, stored)
    outgoing_back = back_owned.reshape(own_count, 3, row_devices, rows_here, col_count).transpose(
        2, 0, 1, 3, 4
    )
    returned = regroup(outgoing_back)
    by_slot = returned.reshape(slab_imgs, -1)
    dpicture = jnp.dot(selector.T, by_slot, preferred_element_type=jnp.float32).astype(jnp.bfloat16)
    dpicture = dpicture.reshape(slab_imgs, 3, rows_here, col_count).transpose(1, 0, 2, 3)
    grad_rimmed = padded_2(dpicture, (("rows", 2),), 1)
    grad_padded = jnp.pad(grad_rimmed, ((0, 0), (0, 0), (0, 0), (1, 1)))
    windows = []
    for offset_y in range(3):
        for offset_x in range(3):
            windows.append(
                grad_padded[
                    :,
                    :,
                    2 - offset_y : 2 - offset_y + rows_here,
                    2 - offset_x : 2 - offset_x + col_count,
                ]
            )
    stacked = jnp.stack(windows, axis=1).reshape(27, -1)
    dactive = lax.dot_general(
        stacked, kernel_rows, (((0,), (0,)), ((), ())), preferred_element_type=jnp.float32
    )
    dactive = dactive.reshape(slab_imgs, rows_here, flat_width)
    gated_grad = dactive * slope_silu * gain_flat
    back_sums = rows_total_sum(
        jnp.stack([channel_group_sums(gated_grad), channel_group_sums(gated_grad * normed)])
    )
    back_one = back_sums[0] / count_group
    back_two = back_sums[1] / count_group
    grad_features = spread_flat(inverse) * (
        gated_grad - spread_flat(back_one) - normed * spread_flat(back_two)
    )
    grad_out = grad_features.astype(jnp.bfloat16).reshape(slab_imgs, rows_here, 1, flat_width)
    return (grad_out, rewards)


def solution(mesh):
    placed = (
        P(("grp", "img"), "rows", "tp", None),
        P("tp"),
        P(None, None, None, "tp"),
        P("rows", None),
        P(),
        P(),
        P("rows", None, "tp"),
        P("rows", "tp"),
        P(),
        P(),
        P(("grp", "img"), None),
    )
    return jax.shard_map(
        body,
        mesh=mesh,
        in_specs=placed,
        out_specs=(P(("grp", "img"), "rows", "tp", None), P(("grp", "img", "rows"))),
        check_vma=False,
    )
```

profile of v0, /device:TPU:0, one launch (start us, length us, event | category | flops | bytes accessed | tf_op | source)
XLA Modules:
  0.0 287.5 jit_solution(1016339752901137906)
XLA Ops:
  7.2 0.7 all-gather.4.cloned.1.call-update
  8.0 0.7 all-gather.6.cloned.1.call-update
  8.7 0.4 convert_reduce_fusion
  9.5 0.4 fusion.22
  10.3 13.6 %psum.37 = f32[2,4,16]{2,1,0:T(4,128)S(1)} all-reduce(f32[2,4,16]{2,1,0:T(4,128)S(1)} %pad_maximum_fusion.2), channel_id=1, replica_groups=mesh['grp'=2,'rows'=4,'img'=2,'tp'=2] {'rows'}, use_global_device_ids=true, to_apply=%region_6.0 | all-reduce | flops 128 | bytes 1024 | tf_op jit(solution)/shard_map/psum | solution.py:97
  24.6 0.3 fusion.32
  25.0 0.4 pad.30
  25.4 0.8 reshape.366
  26.3 0.6 convolution_bitcast_fusion
  26.9 1.2 reshape.368
  28.1 0.2 fusion.67
  28.3 1.3 collective-permute-start
  29.6 1.3 collective-permute-start.1
  31.0 4.7 %collective-permute-done.1 = f32[3,4,1,112]{3,2,1,0:T(1,128)S(1)} collective-permute-done((f32[3,4,1,112]{3,2,1,0:T(1,128)S(1)}, f32[3,4,1,112]{3,2,1,0:T(1,128)S(1)}, u32[]{:S(2)}, u32[]{:S(2)}) %collective-permute-start.1) | collective-permute-done | bytes 5408 | tf_op jit(solution)/shard_map/ppermute | solution.py:24
  36.0 3.4 %psum.38 = bf16[4,2352]{1,0:T(4,128)(2,1)S(1)} all-reduce(bf16[4,2352]{1,0:T(4,128)(2,1)S(1)} %reshape.369), channel_id=1, replica_groups=mesh['grp'=2,'rows'=4,'img'=2,'tp'=2] {'tp'}, use_global_device_ids=true, to_apply=%region_7.8 | all-reduce | flops 9408 | bytes 37632 | tf_op jit(solution)/shard_map/psum | solution.py:101
  39.5 0.7 reshape.370
  40.2 3.3 %all-to-all-start = ((bf16[4,1,3,7,112]{4,3,2,1,0:T(8,128)(2,1)}), bf16[4,1,3,7,112]{4,3,2,1,0:T(8,128)(2,1)S(1)}, u32[]{:S(2)}, u32[]{:S(2)}) async-start(bf16[4,1,3,7,112]{4,3,2,1,0:T(8,128)(2,1)} %bitcast.9), calls=%async_computation | async-start | bytes 49152 | tf_op jit(solution)/shard_map/all_to_all | solution.py:105
  43.6 5.6 %all-to-all-done = bf16[4,1,3,7,112]{4,3,2,1,0:T(8,128)(2,1)S(1)} async-done(((bf16[4,1,3,7,112]{4,3,2,1,0:T(8,128)(2,1)}), bf16[4,1,3,7,112]{4,3,2,1,0:T(8,128)(2,1)S(1)}, u32[]{:S(2)}, u32[]{:S(2)}) %all-to-all-start) | async-done | bytes 18848 | tf_op jit(solution)/shard_map/all_to_all | solution.py:105
  49.2 0.4 reshape.371
  49.6 0.6 copy.48
  50.5 0.7 all-gather.4.cloned.1.call-done
  51.1 2.3 fusion.56
  53.4 0.5 fusion.126
  54.3 89.8 %all-gather.6.cloned.1.call-done = bf16[1280,3,640]{2,0,1:T(8,128)(2,1)} async-done(((bf16[320,3,640]{2,0,1:T(8,128)(2,1)}), bf16[1280,3,640]{2,0,1:T(8,128)(2,1)}) %all-gather.6.cloned.1.call-update) | async-done | bytes 4915216 | tf_op jit(solution)/shard_map/all_gather | solution.py:195
  144.2 1.8 fusion.20
  146.2 1.9 fusion.19
  148.3 0.2 fusion.127
  148.6 1.9 fusion.21
  150.7 0.2 fusion.15
  151.0 0.8 convert_element_type.190
  151.8 30.6 %all-gather.8.cloned.1.call-done = bf16[1280,640]{1,0:T(8,128)(2,1)} async-done(((bf16[320,640]{1,0:T(8,128)(2,1)}), bf16[1280,640]{1,0:T(8,128)(2,1)}) %all-gather.8.cloned.1.call-update) | async-done | bytes 1638416 | tf_op jit(solution)/shard_map/all_gather | solution.py:196
  182.4 2.9 convolution_convert_fusion.2
  185.3 0.2 all-reduce.8.cloned.1.call-start
  185.5 16.8 %all-reduce.6.cloned.1.call-done = bf16[64,1280]{1,0:T(8,128)(2,1)} async-done(((bf16[64,1280]{1,0:T(8,128)(2,1)}), bf16[64,1280]{1,0:T(8,128)(2,1)}) %all-reduce.6.cloned.1.call-update) | async-done | bytes 163856 | tf_op jit(solution)/shard_map/while/body/eval_jaxpr/psum | solution.py:101
  202.3 1.0 add_reduce_fusion
  203.3 0.6 multiply_reduce_fusion.6
  204.5 0.6 multiply_reduce_fusion.5
  205.8 1.9 multiply_reduce_fusion.3
  209.0 1.3 fusion.123
  210.3 0.3 convolution_reduce_fusion
  210.9 1.1 fusion.60
  212.0 1.2 fusion.12
  213.4 0.2 fusion.16
  214.4 2.0 fusion.4
  216.4 2.0 convolution_add_fusion.1
  218.5 2.7 fusion.2
  221.2 19.3 %all-reduce.8.cloned.1.call-done = bf16[64,1280]{1,0:T(8,128)(2,1)} async-done(((bf16[64,1280]{1,0:T(8,128)(2,1)}), bf16[64,1280]{1,0:T(8,128)(2,1)}) %all-reduce.8.cloned.1.call-update) | async-done | bytes 163856 | tf_op jit(solution)/shard_map/while/body/eval_jaxpr/psum | solution.py:101
  240.6 1.1 fusion.55
  241.7 1.1 add_convert_fusion
  242.8 0.6 convolution_convert_fusion.7
  243.7 0.6 copy.62
  244.3 0.3 convert_element_type.211
  244.7 10.3 %all_to_all.10 = bf16[4,1,3,7,112]{4,3,2,1,0:T(8,128)(2,1)S(1)} all-to-all(bf16[4,1,3,7,112]{4,3,2,1,0:T(8,128)(2,1)S(1)} %copy.63), channel_id=1, replica_groups=mesh['grp'=2,'rows'=4,'img'=2,'tp'=2] {'rows'}, dimensions={0} | all-to-all | bytes 37632 | tf_op jit(solution)/shard_map/all_to_all | solution.py:105
  255.4 2.6 collective-permute-start.2
  258.0 1.3 collective-permute-start.3
  259.3 4.2 %collective-permute-done.3 = bf16[3,4,1,112]{3,2,0,1:T(2,128)(2,1)S(1)} collective-permute-done((bf16[3,4,1,112]{3,2,0,1:T(2,128)(2,1)S(1)}, bf16[3,4,1,112]{3,2,0,1:T(2,128)(2,1)S(1)}, u32[]{:S(2)}, u32[]{:S(2)}) %collective-permute-start.3) | collective-permute-done | bytes 2720 | tf_op jit(solution)/shard_map/ppermute | solution.py:24
  264.1 0.3 reshape.378
  264.5 0.4 fusion.132
  264.9 1.4 reshape.380
  266.3 0.5 reshape.379
  266.7 2.2 fusion.122
  269.7 8.9 %psum.41 = f32[2,4,16]{2,1,0:T(4,128)S(1)} all-reduce(f32[2,4,16]{2,1,0:T(4,128)S(1)} %pad_maximum_fusion.3), channel_id=1, replica_groups=mesh['grp'=2,'rows'=4,'img'=2,'tp'=2] {'rows'}, use_global_device_ids=true, to_apply=%region_28.29 | all-reduce | flops 128 | bytes 1024 | tf_op jit(solution)/shard_map/psum | solution.py:97
  279.3 0.6 fusion.53
  279.9 1.1 copy.67
  (144 shorter events, 7.1 us)
Async XLA Ops:
  7.2 1.5 copy-start
  7.2 44.0 %all-gather.4.cloned.1.call-start = ((), (), s32[]{:S(2)}) async-start(), calls=%async_computation.2 | async-start | bytes 2048000 | tf_op jit(solution)/shard_map/all_gather | solution.py:197
  7.9 136.3 %all-gather.6.cloned.1.call-start = ((), (), s32[]{:S(2)}) async-start(), calls=%async_computation.3 | async-start | bytes 6144000 | tf_op jit(solution)/shard_map/all_gather | solution.py:195
  8.7 173.7 %all-gather.8.cloned.1.call-start = ((), (), s32[]{:S(2)}) async-start(), calls=%async_computation.4 | async-start | bytes 2048000 | tf_op jit(solution)/shard_map/all_gather | solution.py:196
  9.1 15.4 %copy-start.21 = (f32[64]{0:T(128)S(1)}, f32[64]{0:T(128)}, u32[]{:S(2)}) copy-start(f32[64]{0:T(128)} %param.16) | copy-start | bytes 772
  25.0 1.3 copy-start.13
  26.3 1.8 copy-start.10
  26.9 12.5 %copy-start.19 = (s32[1,4]{1,0:T(1,128)S(1)}, s32[1,4]{1,0:T(1,128)}, u32[]{:S(2)}) copy-start(s32[1,4]{1,0:T(1,128)} %param.25) | copy-start | bytes 52
  28.3 2.6 collective-permute-start
  29.6 6.1 %collective-permute-start.1 = (f32[3,4,1,112]{3,2,1,0:T(1,128)S(1)}, f32[3,4,1,112]{3,2,1,0:T(1,128)S(1)}, u32[]{:S(2)}, u32[]{:S(2)}) collective-permute-start(f32[3,4,1,112]{3,2,1,0:T(1,128)S(1)} %get-tuple-element.136), channel_id=1, source_target_pairs={{4,0},{8,4},{12,8},{5,1},{9,5},{13,9},{6,2},{10,6},{14,10},{7,3},{... | collective-permute-start | bytes 16136 | tf_op jit(solution)/shard_map/ppermute | solution.py:24
  40.2 9.0 %all-to-all-start = ((bf16[4,1,3,7,112]{4,3,2,1,0:T(8,128)(2,1)}), bf16[4,1,3,7,112]{4,3,2,1,0:T(8,128)(2,1)S(1)}, u32[]{:S(2)}, u32[]{:S(2)}) async-start(bf16[4,1,3,7,112]{4,3,2,1,0:T(8,128)(2,1)} %bitcast.9), calls=%async_computation | async-start | bytes 49152 | tf_op jit(solution)/shard_map/all_to_all | solution.py:105
  43.5 158.8 %all-reduce.6.cloned.1.call-start = ((), (), s32[]{:S(2)}) async-start(), calls=%async_computation.5 | async-start | bytes 327680 | tf_op jit(solution)/shard_map/while/body/eval_jaxpr/psum | solution.py:101
  49.6 3.8 %copy-start.8 = (bf16[64,1280]{1,0:T(8,128)(2,1)S(1)}, bf16[64,1280]{1,0:T(8,128)(2,1)}, u32[]{:S(2)}) copy-start(bf16[64,1280]{1,0:T(8,128)(2,1)} %param.19) | copy-start | bytes 491524
  50.5 3.8 %copy-start.9 = (f32[1280]{0:T(1024)S(1)}, f32[1280]{0:T(1024)}, u32[]{:S(2)}) copy-start(f32[1280]{0:T(1024)} %param.20) | copy-start | bytes 15364
  54.0 94.1 %copy-start.14 = (f32[64]{0:T(128)}, f32[64]{0:T(128)S(1)}, u32[]{:S(2)}) copy-start(f32[64]{0:T(128)S(1)} %broadcast_multiply_fusion.2) | copy-start | bytes 772
  54.2 93.9 %copy-start.16 = (f32[64]{0:T(128)}, f32[64]{0:T(128)S(1)}, u32[]{:S(2)}) copy-start(f32[64]{0:T(128)S(1)} %add_rsqrt_fusion) | copy-start | bytes 772
  146.2 2.4 copy-start.3
  148.3 2.2 copy-start.5
  148.5 2.1 copy-start.7
  148.5 2.5 copy-start.18
  150.7 1.1 copy-start.2
  182.4 27.9 %copy-start.1 = (bf16[1280,640]{1,0:T(8,128)(2,1)S(1)}, bf16[1280,640]{1,0:T(8,128)(2,1)}, u32[]{:S(2)}) copy-start(bf16[1280,640]{1,0:T(8,128)(2,1)} %all-gather.8.cloned.1.call-done) | copy-start | bytes 4915204
  185.3 55.3 %all-reduce.8.cloned.1.call-start = ((), (), s32[]{:S(2)}) async-start(), calls=%async_computation.6 | async-start | bytes 327680 | tf_op jit(solution)/shard_map/while/body/eval_jaxpr/psum | solution.py:101
  210.6 2.6 copy-start.4
  210.6 2.8 copy-start.6
  218.4 22.1 %copy-start.15 = (f32[64]{0:T(128)S(1)}, f32[64]{0:T(128)}, u32[]{:S(2)}) copy-start(f32[64]{0:T(128)} %copy-done.14) | copy-start | bytes 772
  218.4 22.1 %copy-start.17 = (f32[64]{0:T(128)S(1)}, f32[64]{0:T(128)}, u32[]{:S(2)}) copy-start(f32[64]{0:T(128)} %copy-done.16) | copy-start | bytes 772
  218.5 23.3 %copy-start.12 = (f32[1280]{0:T(1024)S(1)}, f32[1280]{0:T(1024)}, u32[]{:S(2)}) copy-start(f32[1280]{0:T(1024)} %get-tuple-element.134) | copy-start | bytes 15364
  221.2 33.8 %copy-start.20 = (s32[1,4]{1,0:T(1,128)S(1)}, s32[1,4]{1,0:T(1,128)}, u32[]{:S(2)}) copy-start(s32[1,4]{1,0:T(1,128)} %param.25) | copy-start | bytes 52
  242.8 21.6 %copy-start.11 = (bf16[27,64]{1,0:T(8,128)(2,1)S(1)}, bf16[27,64]{1,0:T(8,128)(2,1)}, u32[]{:S(2)}) copy-start(bf16[27,64]{1,0:T(8,128)(2,1)} %copy-done.10) | copy-start | bytes 10372
  255.4 3.9 %collective-permute-start.2 = (bf16[3,4,1,112]{3,2,0,1:T(2,128)(2,1)S(1)}, bf16[3,4,1,112]{3,2,0,1:T(2,128)(2,1)S(1)}, u32[]{:S(2)}, u32[]{:S(2)}) collective-permute-start(bf16[3,4,1,112]{3,2,0,1:T(2,128)(2,1)S(1)} %get-tuple-element.138), channel_id=1, source_target_pairs={{0,4},{4,8},{8,12},{1,5},{5,9},{9,13},{2,6},{6,10},{10,14},{3,7},{... | collective-permute-start | bytes 8072 | tf_op jit(solution)/shard_map/ppermute | solution.py:21
  258.0 5.5 %collective-permute-start.3 = (bf16[3,4,1,112]{3,2,0,1:T(2,128)(2,1)S(1)}, bf16[3,4,1,112]{3,2,0,1:T(2,128)(2,1)S(1)}, u32[]{:S(2)}, u32[]{:S(2)}) collective-permute-start(bf16[3,4,1,112]{3,2,0,1:T(2,128)(2,1)S(1)} %get-tuple-element.139), channel_id=1, source_target_pairs={{4,0},{8,4},{12,8},{5,1},{9,5},{13,9},{6,2},{10,6},{14,10},{7,3},{... | collective-permute-start | bytes 8072 | tf_op jit(solution)/shard_map/ppermute | solution.py:24
Sparse Core Ops, SparseCore 0:
  9.6 41.5 all-gather.3
  52.7 91.4 all-gather.5
  145.7 36.5 all-gather.7
  185.4 16.8 all-reduce.5
  221.3 19.1 all-reduce.7
where the time goes:
time: 288 us
  waiting for transfers between devices  173 us (60%)
  blocking collectives  36.1 us (13%)
  matrix products  22.4 us (8%)
  between operations  17.2 us (6%)
  local copies, waits for them, and re-layouts  14.3 us (5%)
  other arithmetic  14.2 us (5%)
  starting transfers between devices  10.1 us (4%)
    all_gather x1, waiting for transfers between devices, body(): lax.all_gather(qkv_w, 'rows', axis=0, tiled=True)  89.8 us
    psum x2, waiting for transfers between devices, head_total(): return lax.psum(values.astype(jnp.bfloat16), 'tp').astype(jnp.float32)  36.1 us
    all_gather x1, waiting for transfers between devices, body(): lax.all_gather(out_w, 'rows', axis=0, tiled=True)  30.6 us
    psum x2, blocking collectives, rows_total_sum(): return lax.psum(values, 'rows')  22.4 us
    all_to_all x1, blocking collectives, regroup(): lax.all_to_all(values, 'rows', split_axis=0, concat_axis=0, tiled=True)  10.3 us
    ppermute x2, waiting for transfers between devices, padded_2(): lax.ppermute(lax.slice_in_dim(block, 0, width, axis=dim), axis, backward)  8.91 us
  transfers between devices with their start and end apart: 10, of which 8 were waited for; matrix products, arithmetic and copies ran while one was open for 7% of the time, Pallas kernels for 0%

commit v1 on v0

--- a/solution.py
+++ b/solution.py
@@ -1,3 +1,4 @@
+import functools
 import math
 import jax
 import jax.numpy as jnp
@@ -11,6 +12,13 @@
 W = 112
 EPS_GROUP = 1e-06
 EPS_LAYER = 1e-05
+
+
+def play_object_on_mesh(content, device_axis):
+    return lax.all_gather(content, device_axis).sum(axis=0)
+
+
+cover_surface_over_axis = functools.partial(play_object_on_mesh, device_axis="tp")
 
 
 def padded_2(block, sides, width):
@@ -98,7 +106,7 @@
 
 
 def head_total(values):
-    return lax.psum(values.astype(jnp.bfloat16), "tp").astype(jnp.float32)
+    return cover_surface_over_axis(values.astype(jnp.bfloat16)).astype(jnp.float32)
 
 
 def regroup(values):

time: 288 us -> 253 us (0.88)
  waiting for transfers between devices: 173 us -> 139 us
    psum x2 -> x0, waiting for transfers between devices: 36.1 us -> none  [head_total(): return lax.psum(values.astype(jnp.bfloat16), 'tp').astype(jnp.float32)]
    all_gather x0 -> x3, blocking collectives: none -> 6.23 us  [play_object_on_mesh(): return lax.all_gather(content, device_axis).sum(axis=0)]
    psum x1 -> x0, blocking collectives: 3.41 us -> none  [head_total(): return lax.psum(values.astype(jnp.bfloat16), 'tp').astype(jnp.float32)]
  transfers between devices with their start and end apart: 10 -> 8, of which waited for: 8 -> 6; matrix products, arithmetic and copies ran while one was open for 7% -> 7% of each run, Pallas kernels for 0% -> 0%
where the time goes in v1:
time: 253 us; the launch traced here: 252 us
  waiting for transfers between devices  139 us (55%)
  blocking collectives  36.7 us (15%)
  matrix products  21 us (8%)
  between operations  17.2 us (7%)
  local copies, waits for them, and re-layouts  14.4 us (6%)
  other arithmetic  14.1 us (6%)
  starting transfers between devices  9.85 us (4%)
    all_gather x1, waiting for transfers between devices, body(): lax.all_gather(qkv_w, 'rows', axis=0, tiled=True)  89.8 us
    all_gather x1, waiting for transfers between devices, body(): lax.all_gather(out_w, 'rows', axis=0, tiled=True)  30.6 us
    psum x2, blocking collectives, rows_total_sum(): return lax.psum(values, 'rows')  22.4 us
    ppermute x2, waiting for transfers between devices, padded_2(): lax.ppermute(lax.slice_in_dim(block, 0, width, axis=dim), axis, backward)  8.8 us
    all_to_all x1, blocking collectives, regroup(): lax.all_to_all(values, 'rows', split_axis=0, concat_axis=0, tiled=True)  7.99 us
    all_gather x3, blocking collectives, play_object_on_mesh(): return lax.all_gather(content, device_axis).sum(axis=0)  6.23 us
    all_to_all x1, waiting for transfers between devices, regroup(): lax.all_to_all(values, 'rows', split_axis=0, concat_axis=0, tiled=True)  6.11 us
  transfers between devices with their start and end apart: 8, of which 6 were waited for; matrix products, arithmetic and copies ran while one was open for 7% of the time, Pallas kernels for 0%

profile of v1, /device:TPU:0, one launch (start us, length us, event | category | flops | bytes accessed | tf_op | source)
XLA Modules:
  0.0 251.9 jit_solution(4043050389631846924)
XLA Ops:
  7.2 0.7 all-gather.7.cloned.1.call-update
  8.0 0.7 all-gather.9.cloned.1.call-update
  8.7 0.4 convert_reduce_fusion
  9.5 0.4 fusion.22
  10.3 13.6 %psum.14 = f32[2,4,16]{2,1,0:T(4,128)S(1)} all-reduce(f32[2,4,16]{2,1,0:T(4,128)S(1)} %pad_maximum_fusion.2), channel_id=1, replica_groups=mesh['grp'=2,'rows'=4,'img'=2,'tp'=2] {'rows'}, use_global_device_ids=true, to_apply=%region_6.0 | all-reduce | flops 128 | bytes 1024 | tf_op jit(solution)/shard_map/psum | solution.py:105
  24.6 0.3 fusion.32
  25.0 0.4 pad.30
  25.4 0.8 reshape.366
  26.3 0.6 convolution_bitcast_fusion
  26.9 1.2 reshape.368
  28.1 0.2 fusion.126
  28.5 1.3 collective-permute-start
  29.8 1.3 collective-permute-start.1
  31.2 4.6 %collective-permute-done.1 = f32[3,4,1,112]{3,1,2,0:T(4,128)S(1)} collective-permute-done((f32[3,4,1,112]{3,1,2,0:T(4,128)S(1)}, f32[3,4,1,112]{3,1,2,0:T(4,128)S(1)}, u32[]{:S(2)}, u32[]{:S(2)}) %collective-permute-start.1) | collective-permute-done | bytes 5408 | tf_op jit(solution)/shard_map/ppermute | solution.py:32
  35.8 1.8 all-gather
  37.9 0.7 reshape.370
  38.6 3.3 %all-to-all-start = ((bf16[4,1,3,7,112]{4,3,2,1,0:T(8,128)(2,1)}), bf16[4,1,3,7,112]{4,3,2,1,0:T(8,128)(2,1)S(1)}, u32[]{:S(2)}, u32[]{:S(2)}) async-start(bf16[4,1,3,7,112]{4,3,2,1,0:T(8,128)(2,1)} %bitcast.10), calls=%async_computation | async-start | bytes 49152 | tf_op jit(solution)/shard_map/all_to_all | solution.py:113
  41.9 6.1 %all-to-all-done = bf16[4,1,3,7,112]{4,3,2,1,0:T(8,128)(2,1)S(1)} async-done(((bf16[4,1,3,7,112]{4,3,2,1,0:T(8,128)(2,1)}), bf16[4,1,3,7,112]{4,3,2,1,0:T(8,128)(2,1)S(1)}, u32[]{:S(2)}, u32[]{:S(2)}) %all-to-all-start) | async-done | bytes 18848 | tf_op jit(solution)/shard_map/all_to_all | solution.py:113
  48.1 0.4 reshape.371
  48.5 0.6 copy.83
  49.3 1.8 all-gather.7.cloned.1.call-done
  51.1 2.3 fusion.56
  53.4 0.5 fusion.129
  54.0 0.2 multiply_reduce_fusion.1
  54.3 89.8 %all-gather.9.cloned.1.call-done = bf16[1280,3,640]{2,0,1:T(8,128)(2,1)} async-done(((bf16[320,3,640]{2,0,1:T(8,128)(2,1)}), bf16[1280,3,640]{2,0,1:T(8,128)(2,1)}) %all-gather.9.cloned.1.call-update) | async-done | bytes 4915216 | tf_op jit(solution)/shard_map/all_gather | solution.py:203
  144.2 1.8 fusion.20
  146.2 1.9 fusion.19
  148.3 0.2 fusion.130
  148.6 1.9 fusion.21
  150.7 0.2 fusion.15
  151.0 0.8 convert_element_type.200
  151.8 30.6 %all-gather.11.cloned.1.call-done = bf16[1280,640]{1,0:T(8,128)(2,1)} async-done(((bf16[320,640]{1,0:T(8,128)(2,1)}), bf16[1280,640]{1,0:T(8,128)(2,1)}) %all-gather.11.cloned.1.call-update) | async-done | bytes 1638416 | tf_op jit(solution)/shard_map/all_gather | solution.py:204
  182.4 2.2 convolution_convert_fusion.2
  184.6 2.4 all-gather.1
  186.9 1.7 reduce_sum.281
  188.7 1.0 add_reduce_fusion
  189.6 0.6 multiply_reduce_fusion.6
  190.9 0.6 multiply_reduce_fusion.5
  192.2 1.9 multiply_reduce_fusion.3
  195.4 1.3 fusion.125
  196.7 0.3 convolution_reduce_fusion
  197.3 1.1 fusion.60
  198.4 1.2 fusion.12
  199.8 0.2 fusion.16
  200.7 2.0 fusion.4
  202.8 2.0 convolution_add_fusion.1
  204.8 2.0 fusion.2
  206.9 2.0 all-gather.2
  209.0 0.2 fusion.55
  209.5 0.6 convolution_convert_fusion.7
  210.3 0.6 copy.97
  210.9 0.3 convert_element_type.221
  211.3 8.0 %all_to_all.10 = bf16[4,1,3,7,112]{4,3,2,1,0:T(8,128)(2,1)S(1)} all-to-all(bf16[4,1,3,7,112]{4,3,2,1,0:T(8,128)(2,1)S(1)} %copy.98), channel_id=1, replica_groups=mesh['grp'=2,'rows'=4,'img'=2,'tp'=2] {'rows'}, dimensions={0} | all-to-all | bytes 37632 | tf_op jit(solution)/shard_map/all_to_all | solution.py:113
  219.7 2.6 %collective-permute-start.2 = (bf16[3,4,1,112]{3,2,0,1:T(2,128)(2,1)S(1)}, bf16[3,4,1,112]{3,2,0,1:T(2,128)(2,1)S(1)}, u32[]{:S(2)}, u32[]{:S(2)}) collective-permute-start(bf16[3,4,1,112]{3,2,0,1:T(2,128)(2,1)S(1)} %get-tuple-element.149), channel_id=1, source_target_pairs={{0,4},{4,8},{8,12},{1,5},{5,9},{9,13},{2,6},{6,10},{10,14},{3,7},{... | collective-permute-start | bytes 8072 | tf_op jit(solution)/shard_map/ppermute | solution.py:29
  222.3 1.3 collective-permute-start.3
  223.7 4.2 %collective-permute-done.3 = bf16[3,4,1,112]{3,2,0,1:T(2,128)(2,1)S(1)} collective-permute-done((bf16[3,4,1,112]{3,2,0,1:T(2,128)(2,1)S(1)}, bf16[3,4,1,112]{3,2,0,1:T(2,128)(2,1)S(1)}, u32[]{:S(2)}, u32[]{:S(2)}) %collective-permute-start.3) | collective-permute-done | bytes 2720 | tf_op jit(solution)/shard_map/ppermute | solution.py:32
  228.4 0.3 reshape.378
  228.8 0.4 fusion.135
  229.2 1.4 reshape.380
  230.6 0.5 reshape.379
  231.1 2.2 fusion.124
  234.1 8.9 %psum.15 = f32[2,4,16]{2,1,0:T(4,128)S(1)} all-reduce(f32[2,4,16]{2,1,0:T(4,128)S(1)} %pad_maximum_fusion.3), channel_id=1, replica_groups=mesh['grp'=2,'rows'=4,'img'=2,'tp'=2] {'rows'}, use_global_device_ids=true, to_apply=%region_28.29 | all-reduce | flops 128 | bytes 1024 | tf_op jit(solution)/shard_map/psum | solution.py:105
  243.6 0.6 fusion.53
  244.2 1.1 copy.102
  (142 shorter events, 7.2 us)
Async XLA Ops:
  7.2 1.5 copy-start
  7.2 44.0 %all-gather.7.cloned.1.call-start = ((), (), s32[]{:S(2)}) async-start(), calls=%async_computation.2 | async-start | bytes 2048000 | tf_op jit(solution)/shard_map/all_gather | solution.py:205
  7.9 136.3 %all-gather.9.cloned.1.call-start = ((), (), s32[]{:S(2)}) async-start(), calls=%async_computation.3 | async-start | bytes 6144000 | tf_op jit(solution)/shard_map/all_gather | solution.py:203
  8.7 173.7 %all-gather.11.cloned.1.call-start = ((), (), s32[]{:S(2)}) async-start(), calls=%async_computation.4 | async-start | bytes 2048000 | tf_op jit(solution)/shard_map/all_gather | solution.py:204
  9.1 15.4 %copy-start.21 = (f32[64]{0:T(128)S(1)}, f32[64]{0:T(128)}, u32[]{:S(2)}) copy-start(f32[64]{0:T(128)} %param.16) | copy-start | bytes 772
  25.0 1.3 copy-start.13
  26.3 1.8 copy-start.10
  28.1 9.7 %copy-start.19 = (s32[1,4]{1,0:T(1,128)S(1)}, s32[1,4]{1,0:T(1,128)}, u32[]{:S(2)}) copy-start(s32[1,4]{1,0:T(1,128)} %param.25) | copy-start | bytes 52
  28.5 2.6 %collective-permute-start = (f32[3,4,1,112]{3,1,2,0:T(4,128)S(1)}, f32[3,4,1,112]{3,1,2,0:T(4,128)S(1)}, u32[]{:S(2)}, u32[]{:S(2)}) collective-permute-start(f32[3,4,1,112]{3,1,2,0:T(4,128)S(1)} %get-tuple-element.148), channel_id=1, source_target_pairs={{0,4},{4,8},{8,12},{1,5},{5,9},{9,13},{2,6},{6,10},{10,14},{3,7},{... | collective-permute-start | bytes 16136 | tf_op jit(solution)/shard_map/ppermute | solution.py:29
  29.8 6.0 %collective-permute-start.1 = (f32[3,4,1,112]{3,1,2,0:T(4,128)S(1)}, f32[3,4,1,112]{3,1,2,0:T(4,128)S(1)}, u32[]{:S(2)}, u32[]{:S(2)}) collective-permute-start(f32[3,4,1,112]{3,1,2,0:T(4,128)S(1)} %get-tuple-element.147), channel_id=1, source_target_pairs={{4,0},{8,4},{12,8},{5,1},{9,5},{13,9},{6,2},{10,6},{14,10},{7,3},{... | collective-permute-start | bytes 16136 | tf_op jit(solution)/shard_map/ppermute | solution.py:32
  38.6 9.4 %all-to-all-start = ((bf16[4,1,3,7,112]{4,3,2,1,0:T(8,128)(2,1)}), bf16[4,1,3,7,112]{4,3,2,1,0:T(8,128)(2,1)S(1)}, u32[]{:S(2)}, u32[]{:S(2)}) async-start(bf16[4,1,3,7,112]{4,3,2,1,0:T(8,128)(2,1)} %bitcast.10), calls=%async_computation | async-start | bytes 49152 | tf_op jit(solution)/shard_map/all_to_all | solution.py:113
  48.5 4.9 %copy-start.8 = (bf16[64,1280]{1,0:T(8,128)(2,1)S(1)}, bf16[64,1280]{1,0:T(8,128)(2,1)}, u32[]{:S(2)}) copy-start(bf16[64,1280]{1,0:T(8,128)(2,1)} %param.19) | copy-start | bytes 491524
  49.3 4.9 %copy-start.9 = (f32[1280]{0:T(1024)S(1)}, f32[1280]{0:T(1024)}, u32[]{:S(2)}) copy-start(f32[1280]{0:T(1024)} %param.20) | copy-start | bytes 15364
  54.0 94.1 %copy-start.14 = (f32[64]{0:T(128)}, f32[64]{0:T(128)S(1)}, u32[]{:S(2)}) copy-start(f32[64]{0:T(128)S(1)} %broadcast_multiply_fusion.2) | copy-start | bytes 772
  54.2 93.9 %copy-start.16 = (f32[64]{0:T(128)}, f32[64]{0:T(128)S(1)}, u32[]{:S(2)}) copy-start(f32[64]{0:T(128)S(1)} %add_rsqrt_fusion) | copy-start | bytes 772
  146.2 2.4 copy-start.3
  148.3 2.2 copy-start.5
  148.5 2.1 copy-start.7
  148.5 2.5 copy-start.18
  150.7 1.1 copy-start.2
  182.4 14.3 %copy-start.1 = (bf16[1280,640]{1,0:T(8,128)(2,1)S(1)}, bf16[1280,640]{1,0:T(8,128)(2,1)}, u32[]{:S(2)}) copy-start(bf16[1280,640]{1,0:T(8,128)(2,1)} %all-gather.11.cloned.1.call-done) | copy-start | bytes 4915204
  197.0 2.6 %copy-start.4 = (bf16[64,8,80]{2,1,0:T(8,128)(2,1)S(1)}, bf16[64,8,80]{2,1,0:T(8,128)(2,1)}, u32[]{:S(2)}) copy-start(bf16[64,8,80]{2,1,0:T(8,128)(2,1)} %copy-done.3) | copy-start | bytes 245764
  197.0 2.8 %copy-start.6 = (bf16[64,8,80]{2,1,0:T(8,128)(2,1)S(1)}, bf16[64,8,80]{2,1,0:T(8,128)(2,1)}, u32[]{:S(2)}) copy-start(bf16[64,8,80]{2,1,0:T(8,128)(2,1)} %copy-done.5) | copy-start | bytes 245764
  204.8 4.2 %copy-start.15 = (f32[64]{0:T(128)S(1)}, f32[64]{0:T(128)}, u32[]{:S(2)}) copy-start(f32[64]{0:T(128)} %copy-done.14) | copy-start | bytes 772
  204.8 4.2 %copy-start.17 = (f32[64]{0:T(128)S(1)}, f32[64]{0:T(128)}, u32[]{:S(2)}) copy-start(f32[64]{0:T(128)} %copy-done.16) | copy-start | bytes 772
  204.8 4.4 %copy-start.12 = (f32[1280]{0:T(1024)S(1)}, f32[1280]{0:T(1024)}, u32[]{:S(2)}) copy-start(f32[1280]{0:T(1024)} %get-tuple-element.136) | copy-start | bytes 15364
  209.0 10.4 %copy-start.20 = (s32[1,4]{1,0:T(1,128)S(1)}, s32[1,4]{1,0:T(1,128)}, u32[]{:S(2)}) copy-start(s32[1,4]{1,0:T(1,128)} %param.25) | copy-start | bytes 52
  209.5 19.3 %copy-start.11 = (bf16[27,64]{1,0:T(8,128)(2,1)S(1)}, bf16[27,64]{1,0:T(8,128)(2,1)}, u32[]{:S(2)}) copy-start(bf16[27,64]{1,0:T(8,128)(2,1)} %copy-done.10) | copy-start | bytes 10372
  219.7 3.9 %collective-permute-start.2 = (bf16[3,4,1,112]{3,2,0,1:T(2,128)(2,1)S(1)}, bf16[3,4,1,112]{3,2,0,1:T(2,128)(2,1)S(1)}, u32[]{:S(2)}, u32[]{:S(2)}) collective-permute-start(bf16[3,4,1,112]{3,2,0,1:T(2,128)(2,1)S(1)} %get-tuple-element.149), channel_id=1, source_target_pairs={{0,4},{4,8},{8,12},{1,5},{5,9},{9,13},{2,6},{6,10},{10,14},{3,7},{... | collective-permute-start | bytes 8072 | tf_op jit(solution)/shard_map/ppermute | solution.py:29
  222.3 5.5 %collective-permute-start.3 = (bf16[3,4,1,112]{3,2,0,1:T(2,128)(2,1)S(1)}, bf16[3,4,1,112]{3,2,0,1:T(2,128)(2,1)S(1)}, u32[]{:S(2)}, u32[]{:S(2)}) collective-permute-start(bf16[3,4,1,112]{3,2,0,1:T(2,128)(2,1)S(1)} %get-tuple-element.150), channel_id=1, source_target_pairs={{4,0},{8,4},{12,8},{5,1},{9,5},{13,9},{6,2},{10,6},{14,10},{7,3},{... | collective-permute-start | bytes 8072 | tf_op jit(solution)/shard_map/ppermute | solution.py:32
Sparse Core Ops, SparseCore 0:
  9.6 41.5 all-gather.6
  52.7 91.4 all-gather.8
  145.7 36.5 all-gather.10
